TPU v7x, 32 devices: a whole 2x2x4 slice. The times are simulated.
32 devices in a mesh: ops: 4 (over z), sec: 8 (over y, x, core).
Axes of the slice: x: 2, y: 2, z: 4, core: 2. Of those that a mesh axis runs over, the one named last changes fastest.
Arguments:
- wavefunction: float32 [512, 128, 128], P(('ops', 'sec')), may hold values from -6 to 6
- left_sector: int32 [512], P(('ops', 'sec')), may hold values from 0 to 15, as said below
- right_sector: int32 [512], P(('ops', 'sec')), may hold values from 0 to 1
- left_size: int32 [16], replicated, may hold values from 64 to 128
- right_size: int32 [2], replicated, may hold values from 64 to 128
- left_ops: float32 [16, 4, 128, 128], P('sec', 'ops'), may hold values from -0.25 to 0.25
- right_ops: float32 [2, 4, 128, 128], P(None, 'ops'), may hold values from -0.5 to 0.5
Outputs:
- sigma: float32 [512, 128, 128], P(('ops', 'sec'))
Inputs may be any that keep to these rules, and one draw needn't show every extreme that they name: `left_sector`: the left sectors of the 16 blocks of one device are distinct and come in whole groups g * 2 to g * 2 + 1.
All inputs are finite; a program needn't handle non-finite values.
Results may differ from a plain program's by a relative error of at most 0.0003.
Values sent between devices are 32-bit elements; how exact they have to be, the bound alone decides.
A program may use at most 64 MiB of HBM per device.

v0:
```python
import jax
import jax.numpy as jnp
from jax import lax
from jax.experimental import pallas as pl
from jax.experimental.pallas import tpu as pltpu
from jax.sharding import PartitionSpec as P

MESH = pl.DeviceIdType.MESH


def contract(running, packed, left_ids, right_ids, live_count, left_blocks, right_blocks):
    turn_count = (live_count + 1) // 2

    def advance(turn_index, current):
        first = 2 * turn_index
        block = lax.dynamic_slice_in_dim(packed, first, 2, 0)
        left_sel = lax.dynamic_slice_in_dim(left_ids, first, 2, 0)
        right_sel = lax.dynamic_slice_in_dim(right_ids, first, 2, 0)
        left_pick = left_blocks[left_sel]
        right_pick = right_blocks[right_sel]
        halfway = jnp.einsum("sij,stlj->stil", block, right_pick, precision=lax.Precision.HIGHEST)
        update = jnp.einsum("stmi,stil->sml", left_pick, halfway, precision=lax.Precision.HIGHEST)
        before = lax.dynamic_slice_in_dim(current, first, 2, 0)
        return lax.dynamic_update_slice_in_dim(current, before + update, first, 0)

    return lax.fori_loop(0, turn_count, advance, running)


def gather_whole(left_ops, right_ops):
    return (
        lax.all_gather(left_ops, "ops", axis=1, tiled=True),
        lax.all_gather(right_ops, "ops", axis=1, tiled=True),
    )


def arrange(incoming, tags, slot_count, width):
    incoming = incoming.reshape(slot_count, width, width)
    tag_ids = tags.reshape(slot_count).astype(jnp.int32)
    live_flag = (tag_ids > 0).astype(jnp.int32)
    order = jnp.argsort(1 - live_flag, stable=True)
    live_count = jnp.sum(live_flag)
    packed = incoming[order]
    right_ids = jnp.maximum(tag_ids[order] - 1, 0)
    return (packed, right_ids, order, live_count)


def shards(wavefunction, left_sector, right_sector, left_size, right_size, left_ops, right_ops):
    peer_count = lax.axis_size("sec")
    sec_local = left_ops.shape[0]
    width = wavefunction.shape[1]
    position = jnp.arange(width)
    left_live = jnp.sum(
        jnp.where(
            left_sector[:, None] == jnp.arange(left_size.shape[0])[None, :], left_size[None, :], 0
        ),
        axis=1,
    )
    right_live = jnp.sum(
        jnp.where(
            right_sector[:, None] == jnp.arange(right_size.shape[0])[None, :],
            right_size[None, :],
            0,
        ),
        axis=1,
    )
    row_live = position[None, :] < left_live[:, None]
    col_live = position[None, :] < right_live[:, None]
    window = (row_live[:, :, None] & col_live[:, None, :]).astype(jnp.float32)
    masked = wavefunction * window
    owner = left_sector // sec_local
    within = left_sector % sec_local
    outgoing = (
        jnp.zeros((peer_count, sec_local, width, width), jnp.float32).at[owner, within].set(masked)
    )
    labels = (
        jnp.zeros((peer_count, sec_local), jnp.float32)
        .at[owner, within]
        .set((right_sector + 1).astype(jnp.float32))
    )
    incoming, tags = (
        lax.all_to_all(outgoing, "sec", split_axis=0, concat_axis=0, tiled=True),
        lax.all_to_all(labels, "sec", split_axis=0, concat_axis=0, tiled=True),
    )
    slot_count = peer_count * sec_local
    packed, right_ids, order, live_count = arrange(incoming, tags, slot_count, width)
    left_ids = order % sec_local
    empty = jnp.zeros_like(packed)
    left_all, right_all = gather_whole(left_ops, right_ops)
    result = contract(empty, packed, left_ids, right_ids, live_count, left_all, right_all)
    restored = jnp.zeros_like(result).at[order].set(result)
    returned = lax.all_to_all(
        restored.reshape(peer_count, sec_local, width, width),
        "sec",
        split_axis=0,
        concat_axis=0,
        tiled=True,
    )
    return returned[owner, within] * window


def term_orders(count):
    orders = []
    for here in range(count):
        orders.append(sorted(range(count), key=lambda t: (abs(t - here), abs(2 * t - count + 1), t)))
    return orders


def split(value):
    high = value.astype(jnp.bfloat16)
    low = (value - high.astype(jnp.float32)).astype(jnp.bfloat16)
    return high, low


def gather_contract(
    wf_hbm, lops_hbm, rops_hbm, lsec, rsec, lsize, rsize,
    out,
    out_ref, out_sem, wbuf, lbuf, rbuf, mcat, hcat, acc, inverse, right_of,
    own_sem, recv_l, recv_r, send_x, send_y, send_up, send_dn, send_sib,
):
    terms = lax.axis_size("ops")
    sectors, _, width, _ = lbuf.shape
    rights = rbuf.shape[1]
    half = width // 2
    z = lax.axis_index("ops")
    sec = lax.axis_index("sec")
    core = sec % 2
    xpos = (sec // 2) % 2
    ypos = sec // 4
    sib = sec + 1 - 2 * core
    xnb = sec + 2 - 4 * xpos
    ynb = sec + 4 - 8 * ypos
    dnb = xnb + 4 - 8 * ypos
    has_up = z < terms - 1
    has_dn = z > 0
    table = term_orders(terms)
    order = []
    for k in range(terms):
        value = table[0][k] * 1
        for here in range(1, terms):
            value = jnp.where(z == here, table[here][k], value)
        order.append(value)

    def flip(group):
        return group + 1 - 2 * core

    barrier = pltpu.get_barrier_semaphore()

    def greet(zz, ss):
        pl.semaphore_signal(barrier, inc=1, device_id=(zz, ss), device_id_type=MESH)

    for peer in (sib, xnb, ynb):
        greet(z, peer)

    @pl.when(has_up)
    def _():
        greet(z + 1, sec)

    @pl.when(has_dn)
    def _():
        greet(z - 1, sec)

    own_l = [
        pltpu.make_async_copy(lops_hbm.at[i, 0], lbuf.at[2 * sec + i, z], recv_l.at[2 * sec + i, z])
        for i in range(2)
    ]
    own_r = pltpu.make_async_copy(rops_hbm.at[:, 0], rbuf.at[z], own_sem.at[0])
    own_w = pltpu.make_async_copy(wf_hbm, wbuf, own_sem.at[1])
    own_w.start()
    own_r.start()
    for copy in own_l:
        copy.start()
    pl.semaphore_wait(barrier, 3 + has_up.astype(jnp.int32) + has_dn.astype(jnp.int32))

    def move(src, dst, ssem, rsem, zz, ss):
        return pltpu.make_async_remote_copy(
            src_ref=src, dst_ref=dst, send_sem=ssem, recv_sem=rsem,
            device_id=(zz, ss), device_id_type=MESH,
        )

    def piece(group, i, t, ssem, zz, ss, own=False):
        s = 2 * group + i
        src = lops_hbm.at[i, 0] if own else lbuf.at[s, t]
        return move(src, lbuf.at[s, t], ssem, recv_l.at[s, t], zz, ss)

    def rpiece(h, t, ssem, zz, ss, own=False):
        rows = pl.ds(pl.multiple_of(h * half, half), half)
        src = rops_hbm.at[:, 0, rows] if own else rbuf.at[t, :, rows]
        return move(src, rbuf.at[t, :, rows], ssem, recv_r.at[t, h], zz, ss)

    def await_l(group, i, t):
        piece(group, i, t, send_x.at[t, 0], z, xnb).wait_recv()

    def await_r(h, t):
        rpiece(h, t, send_x.at[t, 0], z, xnb).wait_recv()

    def along(make, j, t, own, act):
        up = has_up & (t <= z)
        dn = has_dn & (t >= z)

        @pl.when(up)
        def _():
            act(make(t, send_up.at[t, j], z + 1, sec, own))

        @pl.when(dn)
        def _():
            act(make(t, send_dn.at[t, j], z - 1, sec, own))

    def fan_own(i, t, own, act):
        along(lambda t, ssem, zz, ss, own: piece(sec, i, t, ssem, zz, ss, own), i, t, own, act)
        act(piece(sec, i, t, send_x.at[t, i], z, xnb, own))
        act(piece(sec, i, t, send_y.at[t, i], z, ynb, own))
        act(piece(sec, i, t, send_sib.at[t, i], z, sib, own))

    def fan_right(t, own, act):
        along(lambda t, ssem, zz, ss, own: rpiece(core, t, ssem, zz, ss, own), 2, t, own, act)
        if not own:
            act(rpiece(core, t, send_sib.at[t, 8], z, sib))

    def fan_x(i, t, act):
        if i == 0:
            act(piece(xnb, i, t, send_y.at[t, 2], z, ynb))
        act(piece(xnb, i, t, send_sib.at[t, 2 + i], z, sib))

    def fan_y(i, t, act):
        if i == 1:
            act(piece(ynb, i, t, send_x.at[t, 2], z, xnb))
        act(piece(ynb, i, t, send_sib.at[t, 4 + i], z, sib))

    def fan_d(i, t, act):
        act(piece(dnb, i, t, send_sib.at[t, 6 + i], z, sib))

    start = lambda copy: copy.start()
    drain = lambda copy: copy.wait_send()

    t0 = order[0]
    for i in range(2):
        fan_own(i, t0, True, start)
    fan_right(t0, True, start)

    for s in range(sectors):
        value = jnp.int32(0)
        for p in range(1, sectors):
            value = jnp.where(lsec[p] == s, p, value)
        inverse[s] = value
        right_of[s] = rsec[value]

    row_at = lax.broadcasted_iota(jnp.int32, (width, width), 0)
    col_at = lax.broadcasted_iota(jnp.int32, (width, width), 1)

    own_w.wait()

    @pl.loop(0, sectors)
    def _(s):
        live = (row_at < lsize[s]) & (col_at < rsize[right_of[s]])
        high, low = split(jnp.where(live, wbuf[inverse[s]], 0.0))
        rows = pl.ds(pl.multiple_of(s * width, width), width)
        mcat[rows, :width] = high
        mcat[rows, width:] = low
        acc[s] = jnp.zeros((width, width), jnp.float32)

    own_r.wait()
    batch = 4 if sectors % 4 == 0 else 1

    def halfway(t):
        high, low = split(rbuf[t].reshape(rights * width, width))
        doubled = jnp.concatenate([high, high], axis=1)
        contract_last = (((1,), (1,)), ((), ()))

        @pl.loop(0, sectors // batch)
        def _(n):
            rows = pl.ds(pl.multiple_of(n * batch * width, batch * width), batch * width)
            left = mcat[rows, :]
            both = lax.dot_general(left, doubled, contract_last, preferred_element_type=jnp.float32)
            both += lax.dot_general(
                left[:, :width], low, contract_last, preferred_element_type=jnp.float32
            )
            for j in range(batch):
                s = n * batch + j
                mine = both[j * width : (j + 1) * width]
                which = jnp.full((width, width), right_of[s], jnp.int32)
                pick = mine[:, :width]
                for b in range(1, rights):
                    pick = jnp.where(which == b, mine[:, b * width : (b + 1) * width], pick)
                h_high, h_low = split(pick)
                hcat[t, s, :, :width] = h_high
                hcat[t, s, :, width:] = h_low

    def apply_left(s, t):
        high, low = split(lbuf[s, t])
        wide = jnp.dot(
            jnp.concatenate([high, low], axis=0), hcat[t, s], preferred_element_type=jnp.float32
        )
        acc[s] += wide[:width, :width] + (wide[:width, width:] + wide[width:, :width])

    def apply_group(group, t, wait):
        if wait:
            for i in range(2):
                await_l(group, i, t)
        for i in range(2):
            apply_left(2 * group + i, t)

    def land_own(k, i):
        await_l(sec, i, order[k])
        fan_own(i, order[k], False, start)

    def land_side(k, i):
        await_l(xnb, i, order[k])
        fan_x(i, order[k], start)
        await_l(ynb, i, order[k])
        fan_y(i, order[k], start)

    def land_far(k):
        for i in range(2):
            await_l(dnb, i, order[k])
            fan_d(i, order[k], start)

    def land_right(k):
        await_r(core, order[k])
        fan_right(order[k], False, start)

    def apply_side(k):
        apply_group(xnb, order[k], False)
        apply_group(ynb, order[k], False)
        apply_group(flip(xnb), order[k], True)
        apply_group(flip(ynb), order[k], True)

    def apply_far(k):
        apply_group(dnb, order[k], False)
        apply_group(flip(dnb), order[k], True)

    def apply_own(k):
        await_r(1 - core, order[k])
        halfway(order[k])
        apply_group(sec, order[k], False)
        apply_group(sib, order[k], True)

    middle = has_up & has_dn
    border = jnp.logical_not(middle)

    for copy in own_l:
        copy.wait()
    halfway(order[0])
    apply_group(sec, order[0], False)

    for i in range(2):
        land_own(1, i)
        land_side(0, i)

    @pl.when(middle)
    def _():
        for i in range(2):
            land_own(2, i)

    apply_group(sib, order[0], True)
    apply_side(0)
    land_right(1)
    land_side(1, 0)
    apply_own(1)
    land_side(1, 1)

    @pl.when(border)
    def _():
        for i in range(2):
            land_own(2, i)

    @pl.when(middle)
    def _():
        for i in range(2):
            land_own(3, i)
        land_right(2)

    land_far(0)
    apply_side(1)

    @pl.when(border)
    def _():
        for i in range(2):
            land_own(3, i)

    @pl.when(middle)
    def _():
        land_right(3)

    for i in range(2):
        land_side(2, i)
    apply_far(0)

    @pl.when(border)
    def _():
        land_right(2)

    apply_own(2)
    for i in range(2):
        land_side(3, i)
    apply_side(2)

    @pl.when(border)
    def _():
        land_right(3)

    land_far(1)
    apply_own(3)
    apply_far(1)
    land_far(2)
    apply_side(3)
    land_far(3)
    apply_far(2)
    apply_far(3)

    for p in range(sectors):
        s = lsec[p]
        live = (row_at < lsize[s]) & (col_at < rsize[rsec[p]])
        out_ref[p] = jnp.where(live, acc[s], 0.0)
        pltpu.make_async_copy(out_ref.at[p], out.at[p], out_sem.at[p]).start()

    for k in range(terms):
        t = order[k]
        for i in range(2):
            fan_own(i, t, k == 0, drain)
            fan_x(i, t, drain)
            fan_y(i, t, drain)
            fan_d(i, t, drain)
        fan_right(t, k == 0, drain)

    for p in range(sectors):
        pltpu.make_async_copy(out_ref.at[p], out.at[p], out_sem.at[p]).wait()


def local_shards(wavefunction, left_sector, right_sector, left_size, right_size, left_ops, right_ops):
    terms = lax.axis_size("ops")
    sectors, width = left_size.shape[0], wavefunction.shape[1]
    rights = right_size.shape[0]
    dma = pltpu.SemaphoreType.DMA
    anywhere = pl.BlockSpec(memory_space=pl.ANY)
    scalars = pl.BlockSpec(memory_space=pltpu.SMEM)
    return pl.pallas_call(
        gather_contract,
        out_shape=jax.ShapeDtypeStruct(wavefunction.shape, jnp.float32),
        in_specs=[anywhere] * 3 + [scalars] * 4,
        out_specs=anywhere,
        scratch_shapes=[
            pltpu.VMEM(wavefunction.shape, jnp.float32),
            dma((sectors,)),
            pltpu.VMEM((sectors, width, width), jnp.float32),
            pltpu.VMEM((sectors, terms, width, width), jnp.float32),
            pltpu.VMEM((terms, rights, width, width), jnp.float32),
            pltpu.VMEM((sectors * width, 2 * width), jnp.bfloat16),
            pltpu.VMEM((terms, sectors, width, 2 * width), jnp.bfloat16),
            pltpu.VMEM((sectors, width, width), jnp.float32),
            pltpu.SMEM((sectors,), jnp.int32),
            pltpu.SMEM((sectors,), jnp.int32),
            dma((2,)),
            dma((sectors, terms)),
            dma((terms, 2)),
            dma((terms, 3)),
            dma((terms, 3)),
            dma((terms, 3)),
            dma((terms, 3)),
            dma((terms, 9)),
        ],
        compiler_params=pltpu.CompilerParams(collective_id=0, has_side_effects=True),
    )(wavefunction, left_ops, right_ops, left_sector, right_sector, left_size, right_size)


def cube_shards(*arrays):
    wavefunction, left_size, left_ops = arrays[0], arrays[3], arrays[5]
    sectors, width = left_size.shape[0], wavefunction.shape[1]
    terms = lax.axis_size("ops")
    every_sector = wavefunction.shape[0] == sectors
    cube = lax.axis_size("sec") == 2**3 and terms == 2**2 and left_ops.shape[:2] == (2, 1)
    small = sectors * terms * width * width * 4 <= 2**23
    if every_sector and cube and small:
        return local_shards(*arrays)
    return shards(*arrays)


def solution(mesh):
    placed = (
        P(("ops", "sec"), None, None),
        P(("ops", "sec")),
        P(("ops", "sec")),
        P(),
        P(),
        P("sec", "ops", None, None),
        P(None, "ops", None, None),
    )
    return jax.shard_map(
        cube_shards, mesh=mesh, in_specs=placed, out_specs=P(("ops", "sec"), None, None), check_vma=False
    )
```

profile of v0, /device:TPU:1, one launch (start us, length us, event | category | flops | bytes accessed | tf_op | source)
XLA Modules:
  0.0 34.9 jit_solution(6579667101868657176)
XLA Ops:
  0.0 32.6 %shard_map.73 = f32[16,128,128]{2,1,0:T(8,128)} custom-call(f32[16,128,128]{2,1,0:T(8,128)} %wf_hbm.1, f32[2,1,128,128]{3,2,1,0:T(8,128)} %lops_hbm.1, f32[2,1,128,128]{3,2,1,0:T(8,128)} %rops_hbm.1, s32[16]{0:T(128)} %lsec.1, s32[16]{0:T(128)} %rsec.1, s32[16]{0:T(128)} %lsize.1, s32[2]{0:T(128)} %rsize.1), custom_call_target="tpu_custom_call" | custom-call | tf_op jit(solution)/shard_map/pallas_call | solution.py:436
  32.6 2.3 %copy.9 = f32[16,128,128]{2,1,0:T(8,128)} copy(f32[16,128,128]{2,1,0:T(8,128)} %shard_map.73) | data formatting | bytes 2097152
where the time goes:
time: 35.2 us; the launch traced here: 34.9 us
  Pallas kernels  32.6 us (93%)
  local copies, waits for them, and re-layouts  2.3 us (7%)
    pallas_call x1, Pallas kernels, local_shards(): pl.pallas_call(gather_contract, out_shape=jax.ShapeDtypeStruct(wavefuncti...  32.6 us
    unnamed x1, local copies, waits for them, and re-layouts  2.3 us

commit v1 on v0

--- a/solution.py
+++ b/solution.py
@@ -113,8 +113,8 @@
 
 def gather_contract(
     wf_hbm, lops_hbm, rops_hbm, lsec, rsec, lsize, rsize,
-    out,
-    out_ref, out_sem, wbuf, lbuf, rbuf, mcat, hcat, acc, inverse, right_of,
+    out_ref,
+    out_sem, wbuf, lbuf, rbuf, mcat, hcat, acc, inverse, right_of,
     own_sem, recv_l, recv_r, send_x, send_y, send_up, send_dn, send_sib,
 ):
     terms = lax.axis_size("ops")
@@ -411,7 +411,6 @@
         s = lsec[p]
         live = (row_at < lsize[s]) & (col_at < rsize[rsec[p]])
         out_ref[p] = jnp.where(live, acc[s], 0.0)
-        pltpu.make_async_copy(out_ref.at[p], out.at[p], out_sem.at[p]).start()
 
     for k in range(terms):
         t = order[k]
@@ -421,9 +420,6 @@
             fan_y(i, t, drain)
             fan_d(i, t, drain)
         fan_right(t, k == 0, drain)
-
-    for p in range(sectors):
-        pltpu.make_async_copy(out_ref.at[p], out.at[p], out_sem.at[p]).wait()
 
 
 def local_shards(wavefunction, left_sector, right_sector, left_size, right_size, left_ops, right_ops):
@@ -435,13 +431,12 @@
     scalars = pl.BlockSpec(memory_space=pltpu.SMEM)
     return pl.pallas_call(
         gather_contract,
-        out_shape=jax.ShapeDtypeStruct(wavefunction.shape, jnp.float32),
-        in_specs=[anywhere] * 3 + [scalars] * 4,
-        out_specs=anywhere,
+        out_shape=pltpu.VMEM(wavefunction.shape, jnp.float32),
+        in_specs=[pl.BlockSpec(memory_space=pltpu.HBM)] * 3 + [scalars] * 4,
+        out_specs=pl.BlockSpec(memory_space=pltpu.VMEM),
         scratch_shapes=[
+            dma((sectors,)),
             pltpu.VMEM(wavefunction.shape, jnp.float32),
-            dma((sectors,)),
-            pltpu.VMEM((sectors, width, width), jnp.float32),
             pltpu.VMEM((sectors, terms, width, width), jnp.float32),
             pltpu.VMEM((terms, rights, width, width), jnp.float32),
             pltpu.VMEM((sectors * width, 2 * width), jnp.bfloat16),
@@ -458,8 +453,8 @@
             dma((terms, 3)),
             dma((terms, 9)),
         ],
-        compiler_params=pltpu.CompilerParams(collective_id=0, has_side_effects=True),
-    )(wavefunction, left_ops, right_ops, left_sector, right_sector, left_size, right_size)
+        compiler_params=pltpu.CompilerParams(collective_id=0, has_side_effects=True, vmem_limit_bytes=40*2**20),
+    )(*[pltpu.with_memory_space_constraint(a, pltpu.HBM) for a in (wavefunction, left_ops, right_ops, left_sector, right_sector, left_size, right_size)])
 
 
 def cube_shards(*arrays):

time: 35.2 us -> 33.2 us (0.943)
  local copies, waits for them, and re-layouts: 2.3 us -> 0.97 us
  Pallas kernels: 32.6 us -> 31.9 us
    unnamed x1, local copies, waits for them, and re-layouts: 2.3 us -> 0.97 us
    pallas_call x1, Pallas kernels: 32.6 us -> 31.9 us  [local_shards(): pl.pallas_call(gather_contract, out_shape=pltpu.VMEM(wavefunction.shape,...]
where the time goes in v1:
time: 33.2 us; the launch traced here: 32.8 us
  Pallas kernels  31.9 us (96%)
  local copies, waits for them, and re-layouts  0.97 us (3%)
    pallas_call x1, Pallas kernels, local_shards(): pl.pallas_call(gather_contract, out_shape=pltpu.VMEM(wavefunction.shape,...  31.9 us
    unnamed x1, local copies, waits for them, and re-layouts  0.97 us

profile of v1, /device:TPU:1, one launch (start us, length us, event | category | flops | bytes accessed | tf_op | source)
XLA Modules:
  0.0 32.8 jit_solution(1202077147638127373)
XLA Ops:
  0.0 31.9 %shard_map.73 = f32[16,128,128]{2,1,0:T(8,128)S(1)} custom-call(f32[16,128,128]{2,1,0:T(8,128)} %wf_hbm.1, f32[2,1,128,128]{3,2,1,0:T(8,128)} %lops_hbm.1, f32[2,1,128,128]{3,2,1,0:T(8,128)} %rops_hbm.1, s32[16]{0:T(128)} %lsec.1, s32[16]{0:T(128)} %rsec.1, s32[16]{0:T(128)} %lsize.1, s32[2]{0:T(128)} %rsize.1), custom_call_target="tpu_custom_call" | custom-call | tf_op jit(solution)/shard_map/pallas_call | solution.py:432
  31.9 1.0 %copy.9 = f32[16,128,128]{2,1,0:T(8,128)} copy(f32[16,128,128]{2,1,0:T(8,128)S(1)} %shard_map.73) | data formatting | bytes 2097152

commit v2 on v1

v2 whole, which is shorter than its diff:
```python
import jax
import jax.numpy as jnp
from jax import lax
from jax.experimental import pallas as pl
from jax.experimental.pallas import tpu as pltpu
from jax.sharding import PartitionSpec as P

MESH = pl.DeviceIdType.MESH


def contract(running, packed, left_ids, right_ids, live_count, left_blocks, right_blocks):
    turn_count = (live_count + 1) // 2

    def advance(turn_index, current):
        first = 2 * turn_index
        block = lax.dynamic_slice_in_dim(packed, first, 2, 0)
        left_sel = lax.dynamic_slice_in_dim(left_ids, first, 2, 0)
        right_sel = lax.dynamic_slice_in_dim(right_ids, first, 2, 0)
        left_pick = left_blocks[left_sel]
        right_pick = right_blocks[right_sel]
        halfway = jnp.einsum("sij,stlj->stil", block, right_pick, precision=lax.Precision.HIGHEST)
        update = jnp.einsum("stmi,stil->sml", left_pick, halfway, precision=lax.Precision.HIGHEST)
        before = lax.dynamic_slice_in_dim(current, first, 2, 0)
        return lax.dynamic_update_slice_in_dim(current, before + update, first, 0)

    return lax.fori_loop(0, turn_count, advance, running)


def gather_whole(left_ops, right_ops):
    return (
        lax.all_gather(left_ops, "ops", axis=1, tiled=True),
        lax.all_gather(right_ops, "ops", axis=1, tiled=True),
    )


def arrange(incoming, tags, slot_count, width):
    incoming = incoming.reshape(slot_count, width, width)
    tag_ids = tags.reshape(slot_count).astype(jnp.int32)
    live_flag = (tag_ids > 0).astype(jnp.int32)
    order = jnp.argsort(1 - live_flag, stable=True)
    live_count = jnp.sum(live_flag)
    packed = incoming[order]
    right_ids = jnp.maximum(tag_ids[order] - 1, 0)
    return (packed, right_ids, order, live_count)


def shards(wavefunction, left_sector, right_sector, left_size, right_size, left_ops, right_ops):
    peer_count = lax.axis_size("sec")
    sec_local = left_ops.shape[0]
    width = wavefunction.shape[1]
    position = jnp.arange(width)
    left_live = jnp.sum(
        jnp.where(
            left_sector[:, None] == jnp.arange(left_size.shape[0])[None, :], left_size[None, :], 0
        ),
        axis=1,
    )
    right_live = jnp.sum(
        jnp.where(
            right_sector[:, None] == jnp.arange(right_size.shape[0])[None, :],
            right_size[None, :],
            0,
        ),
        axis=1,
    )
    row_live = position[None, :] < left_live[:, None]
    col_live = position[None, :] < right_live[:, None]
    window = (row_live[:, :, None] & col_live[:, None, :]).astype(jnp.float32)
    masked = wavefunction * window
    owner = left_sector // sec_local
    within = left_sector % sec_local
    outgoing = (
        jnp.zeros((peer_count, sec_local, width, width), jnp.float32).at[owner, within].set(masked)
    )
    labels = (
        jnp.zeros((peer_count, sec_local), jnp.float32)
        .at[owner, within]
        .set((right_sector + 1).astype(jnp.float32))
    )
    incoming, tags = (
        lax.all_to_all(outgoing, "sec", split_axis=0, concat_axis=0, tiled=True),
        lax.all_to_all(labels, "sec", split_axis=0, concat_axis=0, tiled=True),
    )
    slot_count = peer_count * sec_local
    packed, right_ids, order, live_count = arrange(incoming, tags, slot_count, width)
    left_ids = order % sec_local
    empty = jnp.zeros_like(packed)
    left_all, right_all = gather_whole(left_ops, right_ops)
    result = contract(empty, packed, left_ids, right_ids, live_count, left_all, right_all)
    restored = jnp.zeros_like(result).at[order].set(result)
    returned = lax.all_to_all(
        restored.reshape(peer_count, sec_local, width, width),
        "sec",
        split_axis=0,
        concat_axis=0,
        tiled=True,
    )
    return returned[owner, within] * window


def split(value):
    high = value.astype(jnp.bfloat16)
    low = (value - high.astype(jnp.float32)).astype(jnp.bfloat16)
    return high, low


LAND, SIBLING, ALONG_X, ALONG_Y, ALONG_UP, ALONG_DOWN, RIGHTS, LEFT, SIBLING_LEFT, LAND_SIBLING = range(10)

PROGRAMS = (
    (
        600, 8, 20, 220, 308, 610, 708, 108, 1, 201, 16, 5, 305, 704, 301, 120,
        101, 205, 700, 41, 900, 800, 24, 424, 116, 28, 2, 202, 141, 302, 128, 21,
        221, 9, 428, 102, 12, 6, 109, 306, 601, 720, 121, 105, 17, 206, 117, 309,
        611, 724, 112, 916, 42, 13, 142, 712, 716, 10, 901, 18, 705, 310, 3, 203,
        110, 303, 602, 103, 113, 124, 22, 222, 612, 709, 801, 701, 29, 7, 118, 107,
        106, 717, 718, 25, 702, 710, 207, 307, 122, 14, 129, 917, 817, 43, 143, 722,
        804, 805, 714, 821, 729, 11, 908, 26, 125, 111, 902, 909, 809, 603, 613, 812,
        820, 813, 126, 114, 19, 903, 924, 828, 30, 130, 119, 925, 807, 703, 707, 726,
        806, 730, 803, 706, 728, 816, 802, 713, 824, 27, 127, 15, 910, 810, 918, 818,
        115, 23, 123, 822, 723, 721, 715, 725, 825, 31, 131, 829, 711, 808, 911, 811,
        926, 919, 727, 830, 731, 826, 719, 815, 814, 819, 823, 927, 827, 831,
    ),
    (
        2, 0, 202, 21, 300, 502, 302, 4, 102, 304, 6, 506, 404, 221, 17, 117,
        400, 601, 611, 42, 306, 204, 40, 206, 9, 140, 542, 440, 121, 309, 3, 16,
        203, 503, 10, 142, 600, 103, 310, 116, 18, 7, 106, 507, 109, 610, 602, 104,
        24, 20, 424, 43, 200, 120, 29, 207, 543, 303, 12, 143, 901, 22, 705, 13,
        110, 28, 428, 612, 702, 603, 118, 25, 129, 112, 107, 805, 125, 801, 14, 222,
        11, 307, 113, 710, 122, 100, 27, 527, 124, 26, 613, 8, 108, 114, 720, 916,
        31, 531, 15, 131, 19, 128, 918, 127, 707, 727, 716, 818, 709, 119, 111, 126,
        708, 822, 703, 724, 717, 711, 820, 917, 817, 23, 123, 816, 115, 30, 130, 909,
        927, 903, 910, 810, 731, 706, 725, 919, 803, 911, 813, 704, 718, 807, 719, 821,
        730, 729, 809, 924, 908, 808, 714, 819, 721, 713, 925, 829, 926, 900, 800, 902,
        806, 828, 814, 700, 831, 815, 812, 824, 715, 826, 701, 723, 827, 830, 726, 728,
        823, 804, 802, 811, 712, 825, 722,
    ),
    (
        3, 503, 303, 203, 602, 612, 10, 110, 103, 1, 5, 405, 7, 18, 305, 201,
        507, 401, 43, 105, 301, 205, 41, 118, 143, 441, 543, 22, 107, 11, 222, 207,
        111, 19, 307, 141, 4, 310, 404, 603, 601, 21, 9, 613, 0, 300, 119, 122,
        903, 221, 200, 104, 400, 14, 13, 27, 527, 309, 204, 121, 304, 113, 702, 40,
        127, 440, 114, 17, 30, 31, 531, 23, 140, 123, 902, 611, 731, 15, 130, 109,
        131, 26, 126, 600, 719, 24, 124, 117, 100, 910, 810, 918, 424, 803, 16, 28,
        101, 116, 726, 610, 716, 428, 8, 25, 901, 29, 115, 806, 728, 703, 927, 707,
        706, 714, 108, 919, 819, 900, 128, 704, 717, 831, 804, 722, 710, 20, 125, 917,
        817, 12, 721, 713, 821, 718, 112, 911, 926, 120, 924, 827, 705, 802, 805, 814,
        708, 129, 909, 813, 709, 818, 725, 727, 720, 724, 715, 908, 800, 826, 730, 808,
        809, 723, 916, 816, 801, 701, 820, 811, 925, 825, 829, 824, 830, 823, 712, 807,
        729, 815, 711, 812, 700, 828, 822,
    ),
    (
        603, 11, 311, 23, 223, 613, 2, 6, 202, 19, 123, 206, 111, 106, 306, 42,
        27, 527, 15, 119, 127, 142, 102, 302, 115, 31, 131, 5, 205, 531, 305, 10,
        110, 731, 22, 1, 222, 711, 301, 310, 903, 41, 201, 911, 141, 602, 612, 105,
        101, 14, 4, 13, 204, 927, 719, 304, 21, 601, 611, 703, 815, 121, 0, 701,
        114, 221, 18, 17, 901, 300, 30, 122, 9, 309, 109, 26, 200, 130, 118, 40,
        140, 117, 721, 805, 722, 715, 807, 727, 803, 718, 710, 705, 104, 600, 702, 126,
        20, 120, 113, 610, 24, 12, 910, 112, 917, 821, 100, 124, 29, 926, 830, 817,
        827, 902, 918, 707, 810, 814, 826, 801, 806, 919, 819, 16, 116, 900, 28, 129,
        8, 128, 25, 108, 804, 811, 822, 823, 725, 700, 125, 916, 704, 729, 726, 730,
        800, 816, 723, 728, 820, 724, 712, 818, 924, 824, 720, 717, 802, 925, 909, 908,
        813, 809, 828, 825, 706, 829, 808, 831, 713, 709, 812, 708, 714, 716,
    ),
)


def gather_contract(
    wf_hbm, lops_hbm, rops_hbm, lsec_hbm, rsec_hbm, lsize_hbm, rsize_hbm,
    out_ref,
    wbuf, lbuf, rbuf, mcat, hcat, acc, lsec, rsec, lsize, rsize, inverse, right_of,
    own_sem, recv_own, recv_sib, recv_r, sends, entered,
):
    terms = lax.axis_size("ops")
    sectors, _, width, _ = lbuf.shape
    rights = rbuf.shape[1]
    half = width // 2
    z = lax.axis_index("ops")
    sec = lax.axis_index("sec")
    core = sec % 2
    xpos = (sec // 2) % 2
    ypos = sec // 4
    sib = sec + 1 - 2 * core
    xnb = sec + 2 - 4 * xpos
    ynb = sec + 4 - 8 * ypos
    dnb = xnb + 4 - 8 * ypos
    has_up = z < terms - 1
    has_dn = z > 0

    def flip(group):
        return group + 1 - 2 * core

    barrier = pltpu.get_barrier_semaphore()

    def greet(sem, zz, ss):
        pl.semaphore_signal(sem, inc=1, device_id=(zz, ss), device_id_type=MESH)

    links = (
        (xpos == 0, xpos == 1, z, xnb),
        (ypos == 0, ypos == 1, z, ynb),
        (has_up, has_dn, z, sec),
        (core == 1, core == 0, z, sib),
    )
    for k, (first, second, zz, ss) in enumerate(links):
        @pl.when(first)
        def _(k=k, zz=zz, ss=ss):
            greet(barrier, zz + 1 if k == 2 else zz, ss)

    scalar_in = [
        pltpu.make_async_copy(src, dst, own_sem.at[2 + n])
        for n, (src, dst) in enumerate(
            ((lsec_hbm, lsec), (rsec_hbm, rsec), (lsize_hbm, lsize), (rsize_hbm, rsize))
        )
    ]
    own_l = [
        pltpu.make_async_copy(lops_hbm.at[i, 0], lbuf.at[2 * sec + i, z], recv_own.at[0, i, z])
        for i in range(2)
    ]
    own_r = pltpu.make_async_copy(rops_hbm.at[:, 0], rbuf.at[z], own_sem.at[0])
    own_w = pltpu.make_async_copy(wf_hbm, wbuf, own_sem.at[1])
    for copy in scalar_in:
        copy.start()
    own_w.start()
    own_r.start()
    for copy in own_l:
        copy.start()
    firsts = xpos + ypos + has_dn.astype(jnp.int32) + 1 - core

    @pl.when(firsts > 0)
    def _():
        pl.semaphore_wait(barrier, firsts)

    for k, (first, second, zz, ss) in enumerate(links):
        @pl.when(second)
        def _(k=k, zz=zz, ss=ss):
            greet(entered.at[k], zz - 1 if k == 2 else zz, ss)

    def move(src, dst, ssem, rsem, zz, ss):
        return pltpu.make_async_remote_copy(
            src_ref=src, dst_ref=dst, send_sem=ssem, recv_sem=rsem,
            device_id=(zz, ss), device_id_type=MESH,
        )

    def piece(group, i, t, link, rsem, zz, ss, own=False):
        s = 2 * group + i
        src = lops_hbm.at[i, 0] if own else lbuf.at[s, t]
        return move(src, lbuf.at[s, t], sends.at[link], rsem, zz, ss)

    def rpiece(h, t, link, zz, ss, own=False):
        rows = pl.ds(pl.multiple_of(h * half, half), half)
        src = rops_hbm.at[:, 0, rows] if own else rbuf.at[t, :, rows]
        return move(src, rbuf.at[t, :, rows], sends.at[link], recv_r.at[t, h], zz, ss)

    def await_l(place, i, t):
        group = groups[place]
        piece(group, i, t, 0, recv_own.at[place, i, t], z, xnb).wait_recv()

    def await_pair(place, t):
        first = 2 * flip(groups[place])
        pair = lbuf.at[pl.ds(first, 2), t]
        move(pair, pair, sends.at[0], recv_sib.at[place, t], z, sib).wait_recv()

    def await_r(h, t):
        rpiece(h, t, 0, z, xnb).wait_recv()

    def drain(link, count):
        blocks = wbuf.at[pl.ds(0, count)]
        move(blocks, blocks, sends.at[link], recv_own.at[0, 0, 0], z, xnb).wait_send()

    groups = (sec, xnb, ynb, dnb)
    sides = {ALONG_UP: (2, 1), ALONG_DOWN: (3, -1)}

    def to_z(way, place, i, t, own=False):
        link, step = sides[way]
        return piece(groups[place], i, t, link, recv_own.at[place, i, t], z + step, sec, own)

    def right_z(way, t, own=False):
        link, step = sides[way]
        return rpiece(core, t, link, z + step, sec, own)

    def to_x(place, i, t, own=False):
        return piece(groups[place], i, t, 0, recv_own.at[place + 1, i, t], z, xnb, own)

    def to_y(place, i, t, own=False):
        return piece(groups[place], i, t, 1, recv_own.at[place + 2, i, t], z, ynb, own)

    def to_sib(place, i, t, own=False):
        link = 4 + (place + 1) // 2
        return piece(groups[place], i, t, link, recv_sib.at[place, t], z, sib, own)

    def own_z(way):
        return [to_z(way, 0, 0, z, True), to_z(way, 0, 1, z, True), right_z(way, z, True)]

    own_sends = (
        [to_x(0, 0, z, True), to_x(0, 1, z, True)],
        [to_y(0, 1, z, True), to_y(0, 0, z, True)],
        [to_sib(0, 0, z, True), to_sib(0, 1, z, True)],
    )

    def start(copies):
        for copy in copies:
            copy.start()

    @pl.when(xpos == 1)
    def _():
        start(own_sends[0])

    @pl.when(ypos == 1)
    def _():
        start(own_sends[1])

    @pl.when(has_dn)
    def _():
        start(own_z(ALONG_DOWN))

    @pl.when(core == 0)
    def _():
        start(own_sends[2])

    for copy in scalar_in:
        copy.wait()
    for s in range(sectors):
        value = jnp.int32(0)
        for p in range(1, sectors):
            value = jnp.where(lsec[p] == s, p, value)
        inverse[s] = value
        right_of[s] = rsec[value]

    @pl.when(core == 1)
    def _():
        pl.semaphore_wait(entered.at[3], 1)
        start(own_sends[2])

    @pl.when(xpos == 0)
    def _():
        pl.semaphore_wait(entered.at[0], 1)
        start(own_sends[0])

    @pl.when(ypos == 0)
    def _():
        pl.semaphore_wait(entered.at[1], 1)
        start(own_sends[1])

    @pl.when(has_up)
    def _():
        pl.semaphore_wait(entered.at[2], 1)
        start(own_z(ALONG_UP))

    row_at = lax.broadcasted_iota(jnp.int32, (width, width), 0)
    col_at = lax.broadcasted_iota(jnp.int32, (width, width), 1)

    own_w.wait()

    @pl.loop(0, sectors)
    def _(s):
        live = (row_at < lsize[s]) & (col_at < rsize[right_of[s]])
        high, low_part = split(jnp.where(live, wbuf[inverse[s]], 0.0))
        rows = pl.ds(pl.multiple_of(s * width, width), width)
        mcat[rows, :width] = high
        mcat[rows, width:] = low_part
        acc[s] = jnp.zeros((width, width), jnp.float32)

    own_r.wait()
    for copy in own_l:
        copy.wait()
    batch = sectors // 2

    def halfway(t, part):
        high, low_part = split(rbuf[t].reshape(rights * width, width))
        doubled = jnp.concatenate([high, high], axis=1)
        contract_last = (((1,), (1,)), ((), ()))
        left = mcat[part * batch * width : (part + 1) * batch * width, :]
        both = lax.dot_general(left, doubled, contract_last, preferred_element_type=jnp.float32)
        both += lax.dot_general(
            left[:, :width], low_part, contract_last, preferred_element_type=jnp.float32
        )
        for j in range(batch):
            s = part * batch + j
            mine = both[j * width : (j + 1) * width]
            which = jnp.full((width, width), right_of[s], jnp.int32)
            pick = mine[:, :width]
            for b in range(1, rights):
                pick = jnp.where(which == b, mine[:, b * width : (b + 1) * width], pick)
            h_high, h_low = split(pick)
            hcat[t, s, :, :width] = h_high
            hcat[t, s, :, width:] = h_low

    def apply_left(s, t):
        high, low_part = split(lbuf[s, t])
        wide = jnp.dot(
            jnp.concatenate([high, low_part], axis=0), hcat[t, s], preferred_element_type=jnp.float32
        )
        acc[s] += wide[:width, :width] + (wide[:width, width:] + wide[width:, :width])

    def run(program, here):
        count = [2, 2, 3 * (here < terms - 1), 3 * (here > 0), 2, 0, 0]

        def send(copy, link):
            copy.start()
            count[link] += 1

        for action in program:
            kind, operand = divmod(action, 100)
            link = {ALONG_X: 0, ALONG_Y: 1, ALONG_UP: 2, ALONG_DOWN: 3}.get(kind)
            if kind == RIGHTS:
                part, t = divmod(operand, 10)
                if t != here and part == 0:
                    await_r(1 - core, t)
                halfway(t, part)
                continue
            if operand >= 40:
                t = operand - 40
                if kind == LAND:
                    await_r(core, t)
                elif kind == SIBLING:
                    send(rpiece(core, t, 4, z, sib), 4)
                else:
                    send(right_z(kind, t), link)
                continue
            place, t = divmod(operand, 4)
            place, i = divmod(place, 2)
            if kind == LAND:
                await_l(place, i, t)
            elif kind == SIBLING:
                send(to_sib(place, i, t), 4 + (place + 1) // 2)
            elif kind == ALONG_X:
                send(to_x(place, i, t), link)
            elif kind == ALONG_Y:
                send(to_y(place, i, t), link)
            elif kind in sides:
                send(to_z(kind, place, i, t), link)
            elif kind == LEFT:
                apply_left(2 * groups[place] + i, t)
            elif kind == SIBLING_LEFT:
                apply_left(2 * flip(groups[place]) + i, t)
            else:
                await_pair(place, t)
        for link, copies in enumerate(count):
            if copies > 0:
                drain(link, copies)

    for here in range(terms):
        @pl.when(z == here)
        def _(here=here):
            run(PROGRAMS[here], here)

    for p in range(sectors):
        s = lsec[p]
        live = (row_at < lsize[s]) & (col_at < rsize[rsec[p]])
        out_ref[p] = jnp.where(live, acc[s], 0.0)


def local_shards(wavefunction, left_sector, right_sector, left_size, right_size, left_ops, right_ops):
    terms = lax.axis_size("ops")
    sectors, width = left_size.shape[0], wavefunction.shape[1]
    rights = right_size.shape[0]
    dma = pltpu.SemaphoreType.DMA
    operands = (
        wavefunction, left_ops, right_ops, left_sector, right_sector, left_size, right_size,
    )
    return pl.pallas_call(
        gather_contract,
        out_shape=pltpu.VMEM(wavefunction.shape, jnp.float32),
        in_specs=[pl.BlockSpec(memory_space=pltpu.HBM)] * 7,
        out_specs=pl.BlockSpec(memory_space=pltpu.VMEM),
        scratch_shapes=[
            pltpu.VMEM(wavefunction.shape, jnp.float32),
            pltpu.VMEM((sectors, terms, width, width), jnp.float32),
            pltpu.VMEM((terms, rights, width, width), jnp.float32),
            pltpu.VMEM((sectors * width, 2 * width), jnp.bfloat16),
            pltpu.VMEM((terms, sectors, width, 2 * width), jnp.bfloat16),
            pltpu.VMEM((sectors, width, width), jnp.float32),
            pltpu.SMEM(left_sector.shape, jnp.int32),
            pltpu.SMEM(right_sector.shape, jnp.int32),
            pltpu.SMEM(left_size.shape, jnp.int32),
            pltpu.SMEM(right_size.shape, jnp.int32),
            pltpu.SMEM((sectors,), jnp.int32),
            pltpu.SMEM((sectors,), jnp.int32),
            dma((6,)),
            dma((4, 2, terms)),
            dma((4, terms)),
            dma((terms, 2)),
            dma((7,)),
            pltpu.SemaphoreType.REGULAR((4,)),
        ],
        compiler_params=pltpu.CompilerParams(collective_id=0, has_side_effects=True, vmem_limit_bytes=40*2**20),
    )(*[pltpu.with_memory_space_constraint(array, pltpu.HBM) for array in operands])


def cube_shards(*arrays):
    wavefunction, left_size, left_ops = arrays[0], arrays[3], arrays[5]
    sectors, width = left_size.shape[0], wavefunction.shape[1]
    terms = lax.axis_size("ops")
    every_sector = wavefunction.shape[0] == sectors
    cube = lax.axis_size("sec") == 2**3 and terms == 2**2 and left_ops.shape[:2] == (2, 1)
    small = sectors * terms * width * width * 4 <= 2**23
    if every_sector and cube and small:
        return local_shards(*arrays)
    return shards(*arrays)


def solution(mesh):
    placed = (
        P(("ops", "sec"), None, None),
        P(("ops", "sec")),
        P(("ops", "sec")),
        P(),
        P(),
        P("sec", "ops", None, None),
        P(None, "ops", None, None),
    )
    return jax.shard_map(
        cube_shards, mesh=mesh, in_specs=placed, out_specs=P(("ops", "sec"), None, None), check_vma=False
    )
```

time: 33.2 us -> 27.1 us (0.82)
  Pallas kernels: 31.9 us -> 26 us
    pallas_call x1, Pallas kernels: 31.9 us -> 26 us  [local_shards(): pl.pallas_call(gather_contract, out_shape=pltpu.VMEM(wavefunction.shape,...]
where the time goes in v2:
time: 27.1 us; the launch traced here: 27 us
  Pallas kernels  26 us (96%)
  local copies, waits for them, and re-layouts  0.97 us (4%)
    pallas_call x1, Pallas kernels, local_shards(): pl.pallas_call(gather_contract, out_shape=pltpu.VMEM(wavefunction.shape,...  26 us
    unnamed x1, local copies, waits for them, and re-layouts  0.97 us

profile of v2, /device:TPU:1, one launch (start us, length us, event | category | flops | bytes accessed | tf_op | source)
XLA Modules:
  0.0 27.0 jit_solution(921121667098014072)
XLA Ops:
  0.0 26.0 %shard_map.73 = f32[16,128,128]{2,1,0:T(8,128)S(1)} custom-call(f32[16,128,128]{2,1,0:T(8,128)} %wf_hbm.1, f32[2,1,128,128]{3,2,1,0:T(8,128)} %lops_hbm.1, f32[2,1,128,128]{3,2,1,0:T(8,128)} %rops_hbm.1, s32[16]{0:T(128)} %lsec_hbm.1, s32[16]{0:T(128)} %rsec_hbm.1, s32[16]{0:T(128)} %lsize_hbm.1, s32[2]{0:T(128)} %rsize_hbm.1), custom_call_target="tpu_custom_call" | custom-call | tf_op jit(solution)/shard_map/pallas_call | solution.py:460
  26.0 1.0 %copy.9 = f32[16,128,128]{2,1,0:T(8,128)} copy(f32[16,128,128]{2,1,0:T(8,128)S(1)} %shard_map.73) | data formatting | bytes 2097152

commit v3 on v2

--- a/solution.py
+++ b/solution.py
@@ -104,62 +104,62 @@
     return high, low
 
 
-LAND, SIBLING, ALONG_X, ALONG_Y, ALONG_UP, ALONG_DOWN, RIGHTS, LEFT, SIBLING_LEFT, LAND_SIBLING = range(10)
+LAND, SIBLING, ALONG_X, ALONG_Y, ALONG_UP, ALONG_DOWN, RIGHTS, LEFT, SIBLING_LEFT, LAND_SIBLING, FAR_END = range(11)
 
 PROGRAMS = (
     (
-        600, 8, 20, 220, 308, 610, 708, 108, 1, 201, 16, 5, 305, 704, 301, 120,
-        101, 205, 700, 41, 900, 800, 24, 424, 116, 28, 2, 202, 141, 302, 128, 21,
-        221, 9, 428, 102, 12, 6, 109, 306, 601, 720, 121, 105, 17, 206, 117, 309,
-        611, 724, 112, 916, 42, 13, 142, 712, 716, 10, 901, 18, 705, 310, 3, 203,
-        110, 303, 602, 103, 113, 124, 22, 222, 612, 709, 801, 701, 29, 7, 118, 107,
-        106, 717, 718, 25, 702, 710, 207, 307, 122, 14, 129, 917, 817, 43, 143, 722,
-        804, 805, 714, 821, 729, 11, 908, 26, 125, 111, 902, 909, 809, 603, 613, 812,
-        820, 813, 126, 114, 19, 903, 924, 828, 30, 130, 119, 925, 807, 703, 707, 726,
-        806, 730, 803, 706, 728, 816, 802, 713, 824, 27, 127, 15, 910, 810, 918, 818,
-        115, 23, 123, 822, 723, 721, 715, 725, 825, 31, 131, 829, 711, 808, 911, 811,
-        926, 919, 727, 830, 731, 826, 719, 815, 814, 819, 823, 927, 827, 831,
+        600, 8, 308, 1, 20, 220, 12, 201, 5, 305, 900, 112, 16, 205, 116, 120,
+        41, 141, 301, 610, 716, 916, 105, 101, 28, 428, 24, 108, 2, 124, 202, 302,
+        21, 424, 221, 6, 306, 908, 601, 704, 720, 708, 712, 9, 206, 309, 901, 17,
+        106, 42, 611, 705, 142, 109, 801, 709, 721, 10, 128, 117, 121, 3, 203, 303,
+        102, 602, 612, 800, 29, 7, 107, 207, 307, 902, 13, 22, 113, 924, 18, 820,
+        728, 713, 718, 310, 103, 110, 917, 222, 816, 710, 700, 804, 701, 129, 14, 43,
+        25, 125, 143, 114, 702, 722, 821, 806, 808, 725, 805, 714, 11, 19, 111, 119,
+        122, 925, 118, 603, 613, 828, 829, 15, 903, 115, 23, 910, 909, 27, 123, 127,
+        918, 812, 707, 727, 814, 810, 822, 803, 703, 809, 818, 729, 825, 717, 911, 30,
+        130, 26, 919, 126, 31, 131, 730, 723, 807, 815, 711, 819, 823, 726, 724, 811,
+        719, 802, 817, 706, 824, 715, 731, 813, 926, 927, 831, 827, 830, 826,
     ),
     (
-        2, 0, 202, 21, 300, 502, 302, 4, 102, 304, 6, 506, 404, 221, 17, 117,
-        400, 601, 611, 42, 306, 204, 40, 206, 9, 140, 542, 440, 121, 309, 3, 16,
-        203, 503, 10, 142, 600, 103, 310, 116, 18, 7, 106, 507, 109, 610, 602, 104,
-        24, 20, 424, 43, 200, 120, 29, 207, 543, 303, 12, 143, 901, 22, 705, 13,
-        110, 28, 428, 612, 702, 603, 118, 25, 129, 112, 107, 805, 125, 801, 14, 222,
-        11, 307, 113, 710, 122, 100, 27, 527, 124, 26, 613, 8, 108, 114, 720, 916,
-        31, 531, 15, 131, 19, 128, 918, 127, 707, 727, 716, 818, 709, 119, 111, 126,
-        708, 822, 703, 724, 717, 711, 820, 917, 817, 23, 123, 816, 115, 30, 130, 909,
-        927, 903, 910, 810, 731, 706, 725, 919, 803, 911, 813, 704, 718, 807, 719, 821,
-        730, 729, 809, 924, 908, 808, 714, 819, 721, 713, 925, 829, 926, 900, 800, 902,
-        806, 828, 814, 700, 831, 815, 812, 824, 715, 826, 701, 723, 827, 830, 726, 728,
-        823, 804, 802, 811, 712, 825, 722,
+        0, 2, 202, 302, 502, 400, 9, 200, 21, 6, 4, 506, 100, 300, 306, 221,
+        404, 40, 309, 204, 140, 42, 542, 601, 17, 18, 440, 142, 3, 503, 901, 104,
+        600, 206, 109, 303, 118, 103, 7, 507, 900, 602, 304, 8, 307, 28, 207, 611,
+        102, 43, 428, 543, 108, 29, 612, 12, 24, 124, 10, 143, 25, 16, 128, 22,
+        107, 310, 203, 122, 13, 125, 424, 113, 106, 121, 610, 702, 924, 718, 706, 728,
+        19, 110, 222, 129, 119, 14, 117, 902, 712, 721, 20, 120, 903, 603, 15, 112,
+        918, 613, 804, 701, 114, 116, 23, 909, 11, 123, 710, 725, 723, 708, 707, 27,
+        115, 925, 127, 703, 813, 704, 916, 824, 26, 30, 130, 31, 126, 806, 131, 805,
+        730, 908, 111, 917, 724, 822, 700, 727, 722, 818, 910, 926, 919, 803, 812, 731,
+        819, 817, 829, 809, 825, 716, 810, 801, 821, 720, 927, 911, 713, 714, 719, 827,
+        814, 815, 820, 711, 816, 811, 826, 830, 715, 807, 800, 828, 808, 831, 802, 709,
+        726, 705, 823, 729, 717,
     ),
     (
-        3, 503, 303, 203, 602, 612, 10, 110, 103, 1, 5, 405, 7, 18, 305, 201,
-        507, 401, 43, 105, 301, 205, 41, 118, 143, 441, 543, 22, 107, 11, 222, 207,
-        111, 19, 307, 141, 4, 310, 404, 603, 601, 21, 9, 613, 0, 300, 119, 122,
-        903, 221, 200, 104, 400, 14, 13, 27, 527, 309, 204, 121, 304, 113, 702, 40,
-        127, 440, 114, 17, 30, 31, 531, 23, 140, 123, 902, 611, 731, 15, 130, 109,
-        131, 26, 126, 600, 719, 24, 124, 117, 100, 910, 810, 918, 424, 803, 16, 28,
-        101, 116, 726, 610, 716, 428, 8, 25, 901, 29, 115, 806, 728, 703, 927, 707,
-        706, 714, 108, 919, 819, 900, 128, 704, 717, 831, 804, 722, 710, 20, 125, 917,
-        817, 12, 721, 713, 821, 718, 112, 911, 926, 120, 924, 827, 705, 802, 805, 814,
-        708, 129, 909, 813, 709, 818, 725, 727, 720, 724, 715, 908, 800, 826, 730, 808,
-        809, 723, 916, 816, 801, 701, 820, 811, 925, 825, 829, 824, 830, 823, 712, 807,
-        729, 815, 711, 812, 700, 828, 822,
+        3, 203, 503, 1, 303, 401, 602, 201, 612, 7, 207, 5, 22, 507, 301, 405,
+        205, 101, 43, 305, 41, 543, 143, 307, 11, 18, 10, 141, 14, 902, 0, 400,
+        603, 441, 300, 122, 613, 310, 222, 9, 107, 111, 110, 4, 118, 304, 114, 105,
+        200, 17, 15, 404, 19, 806, 21, 706, 309, 40, 440, 103, 117, 140, 27, 910,
+        109, 204, 119, 100, 115, 13, 918, 127, 601, 104, 121, 527, 810, 903, 31, 600,
+        221, 901, 16, 113, 23, 30, 131, 531, 28, 710, 428, 611, 714, 909, 123, 731,
+        707, 814, 610, 24, 424, 116, 128, 8, 26, 911, 130, 12, 900, 807, 803, 727,
+        919, 20, 720, 804, 705, 715, 723, 108, 112, 124, 703, 718, 708, 126, 709, 29,
+        25, 801, 722, 813, 818, 129, 927, 120, 125, 908, 926, 721, 712, 800, 717, 724,
+        729, 716, 826, 831, 815, 924, 917, 702, 916, 925, 830, 700, 719, 819, 809, 811,
+        828, 817, 820, 728, 711, 823, 808, 726, 730, 802, 701, 825, 812, 713, 816, 827,
+        805, 824, 704, 829, 725, 821, 822,
     ),
     (
-        603, 11, 311, 23, 223, 613, 2, 6, 202, 19, 123, 206, 111, 106, 306, 42,
-        27, 527, 15, 119, 127, 142, 102, 302, 115, 31, 131, 5, 205, 531, 305, 10,
-        110, 731, 22, 1, 222, 711, 301, 310, 903, 41, 201, 911, 141, 602, 612, 105,
-        101, 14, 4, 13, 204, 927, 719, 304, 21, 601, 611, 703, 815, 121, 0, 701,
-        114, 221, 18, 17, 901, 300, 30, 122, 9, 309, 109, 26, 200, 130, 118, 40,
-        140, 117, 721, 805, 722, 715, 807, 727, 803, 718, 710, 705, 104, 600, 702, 126,
-        20, 120, 113, 610, 24, 12, 910, 112, 917, 821, 100, 124, 29, 926, 830, 817,
-        827, 902, 918, 707, 810, 814, 826, 801, 806, 919, 819, 16, 116, 900, 28, 129,
-        8, 128, 25, 108, 804, 811, 822, 823, 725, 700, 125, 916, 704, 729, 726, 730,
-        800, 816, 723, 728, 820, 724, 712, 818, 924, 824, 720, 717, 802, 925, 909, 908,
-        813, 809, 828, 825, 706, 829, 808, 831, 713, 709, 812, 708, 714, 716,
+        11, 311, 23, 223, 603, 2, 15, 6, 306, 202, 111, 115, 613, 206, 42, 27,
+        302, 527, 142, 1, 31, 531, 19, 201, 101, 301, 22, 711, 123, 119, 5, 127,
+        222, 911, 305, 106, 602, 18, 205, 131, 10, 0, 1027, 310, 200, 122, 1031, 612,
+        9, 14, 102, 927, 811, 903, 41, 309, 109, 118, 831, 17, 141, 919, 727, 710,
+        110, 30, 300, 21, 100, 221, 4, 304, 130, 204, 722, 117, 601, 611, 13, 113,
+        40, 26, 104, 902, 121, 140, 918, 114, 105, 806, 819, 726, 718, 705, 731, 126,
+        815, 807, 701, 715, 702, 802, 714, 707, 730, 823, 600, 723, 8, 910, 909, 25,
+        900, 29, 129, 917, 28, 125, 926, 610, 16, 725, 804, 704, 128, 901, 116, 24,
+        108, 124, 12, 112, 20, 120, 925, 814, 813, 708, 817, 821, 706, 712, 830, 728,
+        822, 810, 729, 721, 713, 829, 809, 724, 825, 826, 924, 916, 908, 816, 818, 827,
+        812, 717, 716, 720, 803, 703, 805, 824, 800, 801, 828, 719, 808, 709, 820, 700,
     ),
 )
 
@@ -272,6 +272,9 @@
     def to_z(way, place, i, t, own=False):
         link, step = sides[way]
         return piece(groups[place], i, t, link, recv_own.at[place, i, t], z + step, sec, own)
+
+    def to_far_end(place, i, t):
+        return piece(groups[place], i, t, 3, recv_own.at[place, i, t], z + 1 - terms, sec)
 
     def right_z(way, t, own=False):
         link, step = sides[way]
@@ -428,6 +431,8 @@
                 send(to_y(place, i, t), link)
             elif kind in sides:
                 send(to_z(kind, place, i, t), link)
+            elif kind == FAR_END:
+                send(to_far_end(place, i, t), 3)
             elif kind == LEFT:
                 apply_left(2 * groups[place] + i, t)
             elif kind == SIBLING_LEFT:

time: 27.1 us -> 26 us (0.959)
  Pallas kernels: 26 us -> 24.9 us
    pallas_call x1, Pallas kernels: 26 us -> 24.9 us  [local_shards(): pl.pallas_call(gather_contract, out_shape=pltpu.VMEM(wavefunction.shape,...]
where the time goes in v3:
time: 26 us; the launch traced here: 25.9 us
  Pallas kernels  24.9 us (96%)
  local copies, waits for them, and re-layouts  0.97 us (4%)
    pallas_call x1, Pallas kernels, local_shards(): pl.pallas_call(gather_contract, out_shape=pltpu.VMEM(wavefunction.shape,...  24.9 us
    unnamed x1, local copies, waits for them, and re-layouts  0.97 us

profile of v3, /device:TPU:1, one launch (start us, length us, event | category | flops | bytes accessed | tf_op | source)
XLA Modules:
  0.0 25.9 jit_solution(2206444205173476595)
XLA Ops:
  0.0 24.9 %shard_map.73 = f32[16,128,128]{2,1,0:T(8,128)S(1)} custom-call(f32[16,128,128]{2,1,0:T(8,128)} %wf_hbm.1, f32[2,1,128,128]{3,2,1,0:T(8,128)} %lops_hbm.1, f32[2,1,128,128]{3,2,1,0:T(8,128)} %rops_hbm.1, s32[16]{0:T(128)} %lsec_hbm.1, s32[16]{0:T(128)} %rsec_hbm.1, s32[16]{0:T(128)} %lsize_hbm.1, s32[2]{0:T(128)} %rsize_hbm.1), custom_call_target="tpu_custom_call" | custom-call | tf_op jit(solution)/shard_map/pallas_call | solution.py:465
  24.9 1.0 %copy.9 = f32[16,128,128]{2,1,0:T(8,128)} copy(f32[16,128,128]{2,1,0:T(8,128)S(1)} %shard_map.73) | data formatting | bytes 2097152

commit v4 on v3

--- a/solution.py
+++ b/solution.py
@@ -151,7 +151,7 @@
     (
         11, 311, 23, 223, 603, 2, 15, 6, 306, 202, 111, 115, 613, 206, 42, 27,
         302, 527, 142, 1, 31, 531, 19, 201, 101, 301, 22, 711, 123, 119, 5, 127,
-        222, 911, 305, 106, 602, 18, 205, 131, 10, 0, 1027, 310, 200, 122, 1031, 612,
+        222, 911, 305, 106, 602, 18, 205, 131, 10, 0, 1027, 1031, 310, 200, 122, 612,
         9, 14, 102, 927, 811, 903, 41, 309, 109, 118, 831, 17, 141, 919, 727, 710,
         110, 30, 300, 21, 100, 221, 4, 304, 130, 204, 722, 117, 601, 611, 13, 113,
         40, 26, 104, 902, 121, 140, 918, 114, 105, 806, 819, 726, 718, 705, 731, 126,
@@ -290,14 +290,15 @@
         link = 4 + (place + 1) // 2
         return piece(groups[place], i, t, link, recv_sib.at[place, t], z, sib, own)
 
-    def own_z(way):
-        return [to_z(way, 0, 0, z, True), to_z(way, 0, 1, z, True), right_z(way, z, True)]
-
-    own_sends = (
-        [to_x(0, 0, z, True), to_x(0, 1, z, True)],
-        [to_y(0, 1, z, True), to_y(0, 0, z, True)],
-        [to_sib(0, 0, z, True), to_sib(0, 1, z, True)],
-    )
+    def own_z(way, own):
+        return [to_z(way, 0, 0, z, own), to_z(way, 0, 1, z, own), right_z(way, z, own)]
+
+    def own_sends(own):
+        return (
+            [to_x(0, 0, z, own), to_x(0, 1, z, own)],
+            [to_y(0, 1, z, own), to_y(0, 0, z, own)],
+            [to_sib(0, 0, z, own), to_sib(0, 1, z, own)],
+        )
 
     def start(copies):
         for copy in copies:
@@ -305,19 +306,19 @@
 
     @pl.when(xpos == 1)
     def _():
-        start(own_sends[0])
+        start(own_sends(True)[0])
 
     @pl.when(ypos == 1)
     def _():
-        start(own_sends[1])
+        start(own_sends(True)[1])
 
     @pl.when(has_dn)
     def _():
-        start(own_z(ALONG_DOWN))
+        start(own_z(ALONG_DOWN, True))
 
     @pl.when(core == 0)
     def _():
-        start(own_sends[2])
+        start(own_sends(True)[2])
 
     for copy in scalar_in:
         copy.wait()
@@ -328,25 +329,29 @@
         inverse[s] = value
         right_of[s] = rsec[value]
 
+    own_r.wait()
+    for copy in own_l:
+        copy.wait()
+
     @pl.when(core == 1)
     def _():
         pl.semaphore_wait(entered.at[3], 1)
-        start(own_sends[2])
+        start(own_sends(False)[2])
 
     @pl.when(xpos == 0)
     def _():
         pl.semaphore_wait(entered.at[0], 1)
-        start(own_sends[0])
+        start(own_sends(False)[0])
 
     @pl.when(ypos == 0)
     def _():
         pl.semaphore_wait(entered.at[1], 1)
-        start(own_sends[1])
+        start(own_sends(False)[1])
 
     @pl.when(has_up)
     def _():
         pl.semaphore_wait(entered.at[2], 1)
-        start(own_z(ALONG_UP))
+        start(own_z(ALONG_UP, False))
 
     row_at = lax.broadcasted_iota(jnp.int32, (width, width), 0)
     col_at = lax.broadcasted_iota(jnp.int32, (width, width), 1)
@@ -362,9 +367,6 @@
         mcat[rows, width:] = low_part
         acc[s] = jnp.zeros((width, width), jnp.float32)
 
-    own_r.wait()
-    for copy in own_l:
-        copy.wait()
     batch = sectors // 2
 
     def halfway(t, part):
@@ -497,6 +499,7 @@
     terms = lax.axis_size("ops")
     every_sector = wavefunction.shape[0] == sectors
     cube = lax.axis_size("sec") == 2**3 and terms == 2**2 and left_ops.shape[:2] == (2, 1)
+    cube = cube and arrays[4].shape[0] == 2
     small = sectors * terms * width * width * 4 <= 2**23
     if every_sector and cube and small:
         return local_shards(*arrays)

time: 26 us -> 26 us (level)
  no operation moved by 1% of the time
where the time goes in v4:
time: 26 us; the launch traced here: 25.9 us
  Pallas kernels  24.9 us (96%)
  local copies, waits for them, and re-layouts  0.97 us (4%)
    pallas_call x1, Pallas kernels, local_shards(): pl.pallas_call(gather_contract, out_shape=pltpu.VMEM(wavefunction.shape,...  24.9 us
    unnamed x1, local copies, waits for them, and re-layouts  0.97 us

profile of v4, /device:TPU:1, one launch (start us, length us, event | category | flops | bytes accessed | tf_op | source)
XLA Modules:
  0.0 25.9 jit_solution(6020208195208310966)
XLA Ops:
  0.0 24.9 %shard_map.73 = f32[16,128,128]{2,1,0:T(8,128)S(1)} custom-call(f32[16,128,128]{2,1,0:T(8,128)} %wf_hbm.1, f32[2,1,128,128]{3,2,1,0:T(8,128)} %lops_hbm.1, f32[2,1,128,128]{3,2,1,0:T(8,128)} %rops_hbm.1, s32[16]{0:T(128)} %lsec_hbm.1, s32[16]{0:T(128)} %rsec_hbm.1, s32[16]{0:T(128)} %lsize_hbm.1, s32[2]{0:T(128)} %rsize_hbm.1), custom_call_target="tpu_custom_call" | custom-call | tf_op jit(solution)/shard_map/pallas_call | solution.py:467
  24.9 1.0 %copy.9 = f32[16,128,128]{2,1,0:T(8,128)} copy(f32[16,128,128]{2,1,0:T(8,128)S(1)} %shard_map.73) | data formatting | bytes 2097152

commit v5 on v4

--- a/solution.py
+++ b/solution.py
@@ -108,58 +108,58 @@
 
 PROGRAMS = (
     (
-        600, 8, 308, 1, 20, 220, 12, 201, 5, 305, 900, 112, 16, 205, 116, 120,
-        41, 141, 301, 610, 716, 916, 105, 101, 28, 428, 24, 108, 2, 124, 202, 302,
-        21, 424, 221, 6, 306, 908, 601, 704, 720, 708, 712, 9, 206, 309, 901, 17,
-        106, 42, 611, 705, 142, 109, 801, 709, 721, 10, 128, 117, 121, 3, 203, 303,
-        102, 602, 612, 800, 29, 7, 107, 207, 307, 902, 13, 22, 113, 924, 18, 820,
-        728, 713, 718, 310, 103, 110, 917, 222, 816, 710, 700, 804, 701, 129, 14, 43,
-        25, 125, 143, 114, 702, 722, 821, 806, 808, 725, 805, 714, 11, 19, 111, 119,
-        122, 925, 118, 603, 613, 828, 829, 15, 903, 115, 23, 910, 909, 27, 123, 127,
-        918, 812, 707, 727, 814, 810, 822, 803, 703, 809, 818, 729, 825, 717, 911, 30,
-        130, 26, 919, 126, 31, 131, 730, 723, 807, 815, 711, 819, 823, 726, 724, 811,
-        719, 802, 817, 706, 824, 715, 731, 813, 926, 927, 831, 827, 830, 826,
+        8, 308, 20, 220, 108, 600, 1, 201, 101, 610, 16, 301, 5, 704, 105, 716,
+        305, 12, 120, 116, 900, 800, 41, 205, 916, 141, 28, 24, 112, 124, 901, 424,
+        2, 202, 302, 428, 128, 816, 720, 601, 908, 17, 6, 206, 924, 306, 9, 611,
+        804, 709, 712, 828, 705, 21, 109, 309, 13, 221, 700, 42, 142, 117, 801, 805,
+        708, 102, 106, 10, 310, 3, 203, 121, 18, 113, 110, 602, 612, 22, 7, 207,
+        307, 14, 118, 222, 909, 122, 917, 902, 722, 813, 706, 29, 107, 129, 103, 25,
+        43, 303, 125, 918, 114, 143, 818, 821, 728, 820, 702, 717, 701, 724, 817, 824,
+        721, 725, 808, 809, 806, 812, 713, 822, 26, 11, 603, 613, 710, 15, 23, 925,
+        111, 910, 31, 903, 115, 126, 123, 814, 802, 703, 723, 731, 803, 131, 30, 19,
+        119, 130, 27, 127, 911, 715, 719, 718, 707, 726, 815, 825, 727, 730, 829, 811,
+        729, 711, 714, 810, 807, 919, 926, 927, 823, 831, 819, 827, 826, 830,
     ),
     (
-        0, 2, 202, 302, 502, 400, 9, 200, 21, 6, 4, 506, 100, 300, 306, 221,
-        404, 40, 309, 204, 140, 42, 542, 601, 17, 18, 440, 142, 3, 503, 901, 104,
-        600, 206, 109, 303, 118, 103, 7, 507, 900, 602, 304, 8, 307, 28, 207, 611,
-        102, 43, 428, 543, 108, 29, 612, 12, 24, 124, 10, 143, 25, 16, 128, 22,
-        107, 310, 203, 122, 13, 125, 424, 113, 106, 121, 610, 702, 924, 718, 706, 728,
-        19, 110, 222, 129, 119, 14, 117, 902, 712, 721, 20, 120, 903, 603, 15, 112,
-        918, 613, 804, 701, 114, 116, 23, 909, 11, 123, 710, 725, 723, 708, 707, 27,
-        115, 925, 127, 703, 813, 704, 916, 824, 26, 30, 130, 31, 126, 806, 131, 805,
-        730, 908, 111, 917, 724, 822, 700, 727, 722, 818, 910, 926, 919, 803, 812, 731,
-        819, 817, 829, 809, 825, 716, 810, 801, 821, 720, 927, 911, 713, 714, 719, 827,
-        814, 815, 820, 711, 816, 811, 826, 830, 715, 807, 800, 828, 808, 831, 802, 709,
-        726, 705, 823, 729, 717,
+        0, 300, 2, 200, 502, 202, 400, 6, 506, 306, 4, 304, 21, 601, 404, 102,
+        104, 206, 106, 42, 142, 221, 542, 9, 611, 204, 13, 40, 709, 3, 109, 440,
+        503, 302, 113, 602, 612, 103, 7, 16, 507, 702, 121, 17, 309, 203, 140, 303,
+        107, 10, 14, 706, 24, 43, 143, 543, 424, 22, 307, 124, 8, 116, 207, 108,
+        20, 100, 114, 600, 713, 28, 902, 29, 128, 110, 428, 310, 901, 120, 222, 117,
+        610, 603, 613, 916, 720, 805, 714, 801, 721, 820, 11, 18, 12, 900, 717, 729,
+        118, 910, 112, 15, 903, 115, 111, 31, 19, 924, 917, 718, 711, 816, 712, 908,
+        812, 803, 25, 122, 119, 125, 30, 129, 909, 26, 716, 126, 23, 130, 817, 708,
+        814, 809, 722, 821, 704, 918, 911, 27, 127, 123, 925, 131, 723, 730, 825, 710,
+        715, 700, 707, 725, 806, 829, 813, 727, 724, 810, 800, 804, 926, 927, 919, 831,
+        828, 703, 823, 808, 719, 827, 731, 830, 815, 818, 726, 705, 802, 811, 822, 826,
+        819, 728, 807, 701, 824,
     ),
     (
-        3, 203, 503, 1, 303, 401, 602, 201, 612, 7, 207, 5, 22, 507, 301, 405,
-        205, 101, 43, 305, 41, 543, 143, 307, 11, 18, 10, 141, 14, 902, 0, 400,
-        603, 441, 300, 122, 613, 310, 222, 9, 107, 111, 110, 4, 118, 304, 114, 105,
-        200, 17, 15, 404, 19, 806, 21, 706, 309, 40, 440, 103, 117, 140, 27, 910,
-        109, 204, 119, 100, 115, 13, 918, 127, 601, 104, 121, 527, 810, 903, 31, 600,
-        221, 901, 16, 113, 23, 30, 131, 531, 28, 710, 428, 611, 714, 909, 123, 731,
-        707, 814, 610, 24, 424, 116, 128, 8, 26, 911, 130, 12, 900, 807, 803, 727,
-        919, 20, 720, 804, 705, 715, 723, 108, 112, 124, 703, 718, 708, 126, 709, 29,
-        25, 801, 722, 813, 818, 129, 927, 120, 125, 908, 926, 721, 712, 800, 717, 724,
-        729, 716, 826, 831, 815, 924, 917, 702, 916, 925, 830, 700, 719, 819, 809, 811,
-        828, 817, 820, 728, 711, 823, 808, 726, 730, 802, 701, 825, 812, 713, 816, 827,
-        805, 824, 704, 829, 725, 821, 822,
+        3, 203, 303, 503, 22, 1, 301, 602, 122, 222, 14, 401, 7, 507, 5, 10,
+        405, 207, 18, 101, 612, 201, 305, 902, 43, 105, 143, 543, 806, 714, 103, 110,
+        41, 307, 141, 118, 0, 400, 702, 205, 441, 603, 17, 11, 100, 4, 30, 310,
+        19, 404, 601, 613, 200, 104, 300, 15, 304, 40, 119, 31, 21, 114, 531, 918,
+        9, 440, 140, 121, 715, 204, 109, 111, 309, 818, 23, 901, 115, 27, 611, 26,
+        221, 13, 24, 424, 8, 731, 113, 527, 600, 127, 124, 117, 108, 28, 16, 911,
+        428, 128, 12, 909, 910, 112, 20, 107, 126, 900, 130, 131, 116, 610, 707, 719,
+        701, 120, 924, 25, 917, 29, 129, 908, 927, 123, 125, 926, 720, 713, 817, 804,
+        709, 810, 711, 703, 710, 718, 724, 723, 808, 801, 903, 916, 726, 827, 725, 830,
+        717, 712, 729, 805, 828, 800, 728, 821, 813, 814, 815, 706, 705, 730, 727, 722,
+        802, 824, 826, 811, 812, 803, 809, 919, 925, 716, 700, 721, 822, 831, 704, 820,
+        708, 823, 819, 825, 829, 807, 816,
     ),
     (
-        11, 311, 23, 223, 603, 2, 15, 6, 306, 202, 111, 115, 613, 206, 42, 27,
-        302, 527, 142, 1, 31, 531, 19, 201, 101, 301, 22, 711, 123, 119, 5, 127,
-        222, 911, 305, 106, 602, 18, 205, 131, 10, 0, 1027, 1031, 310, 200, 122, 612,
-        9, 14, 102, 927, 811, 903, 41, 309, 109, 118, 831, 17, 141, 919, 727, 710,
-        110, 30, 300, 21, 100, 221, 4, 304, 130, 204, 722, 117, 601, 611, 13, 113,
-        40, 26, 104, 902, 121, 140, 918, 114, 105, 806, 819, 726, 718, 705, 731, 126,
-        815, 807, 701, 715, 702, 802, 714, 707, 730, 823, 600, 723, 8, 910, 909, 25,
-        900, 29, 129, 917, 28, 125, 926, 610, 16, 725, 804, 704, 128, 901, 116, 24,
-        108, 124, 12, 112, 20, 120, 925, 814, 813, 708, 817, 821, 706, 712, 830, 728,
-        822, 810, 729, 721, 713, 829, 809, 724, 825, 826, 924, 916, 908, 816, 818, 827,
-        812, 717, 716, 720, 803, 703, 805, 824, 800, 801, 828, 719, 808, 709, 820, 700,
+        903, 603, 23, 223, 11, 311, 2, 302, 102, 613, 202, 707, 15, 6, 206, 123,
+        111, 19, 42, 715, 803, 306, 703, 723, 31, 142, 27, 131, 115, 531, 106, 127,
+        1, 301, 201, 527, 731, 727, 602, 711, 10, 5, 305, 110, 902, 205, 911, 612,
+        310, 815, 22, 806, 0, 1031, 14, 101, 927, 200, 719, 1027, 18, 119, 105, 17,
+        222, 9, 300, 109, 117, 811, 114, 41, 100, 141, 122, 118, 13, 113, 21, 121,
+        807, 706, 4, 204, 304, 919, 601, 221, 26, 901, 909, 40, 140, 104, 8, 126,
+        309, 917, 611, 701, 721, 805, 821, 726, 705, 30, 130, 900, 600, 819, 16, 918,
+        24, 108, 124, 926, 822, 831, 910, 20, 12, 112, 120, 116, 610, 801, 823, 810,
+        713, 720, 818, 702, 814, 29, 28, 25, 916, 908, 128, 125, 129, 718, 708, 717,
+        813, 700, 802, 712, 812, 716, 714, 729, 725, 730, 820, 809, 724, 830, 817, 710,
+        804, 827, 924, 925, 800, 826, 704, 829, 816, 808, 728, 722, 825, 828, 824, 709,
     ),
 )
 

time: 26 us -> 25.7 us (0.988)
  Pallas kernels: 24.9 us -> 24.6 us
    pallas_call x1, Pallas kernels: 24.9 us -> 24.6 us  [local_shards(): pl.pallas_call(gather_contract, out_shape=pltpu.VMEM(wavefunction.shape,...]
where the time goes in v5:
time: 25.7 us; the launch traced here: 25.6 us
  Pallas kernels  24.6 us (96%)
  local copies, waits for them, and re-layouts  0.97 us (4%)
    pallas_call x1, Pallas kernels, local_shards(): pl.pallas_call(gather_contract, out_shape=pltpu.VMEM(wavefunction.shape,...  24.6 us
    unnamed x1, local copies, waits for them, and re-layouts  0.97 us

profile of v5, /device:TPU:1, one launch (start us, length us, event | category | flops | bytes accessed | tf_op | source)
XLA Modules:
  0.0 25.6 jit_solution(6847742686505427968)
XLA Ops:
  0.0 24.6 %shard_map.73 = f32[16,128,128]{2,1,0:T(8,128)S(1)} custom-call(f32[16,128,128]{2,1,0:T(8,128)} %wf_hbm.1, f32[2,1,128,128]{3,2,1,0:T(8,128)} %lops_hbm.1, f32[2,1,128,128]{3,2,1,0:T(8,128)} %rops_hbm.1, s32[16]{0:T(128)} %lsec_hbm.1, s32[16]{0:T(128)} %rsec_hbm.1, s32[16]{0:T(128)} %lsize_hbm.1, s32[2]{0:T(128)} %rsize_hbm.1), custom_call_target="tpu_custom_call" | custom-call | tf_op jit(solution)/shard_map/pallas_call | solution.py:467
  24.6 1.0 %copy.9 = f32[16,128,128]{2,1,0:T(8,128)} copy(f32[16,128,128]{2,1,0:T(8,128)S(1)} %shard_map.73) | data formatting | bytes 2097152

commit v6 on v5

--- a/solution.py
+++ b/solution.py
@@ -320,6 +320,30 @@
     def _():
         start(own_sends(True)[2])
 
+    own_r.wait()
+    for copy in own_l:
+        copy.wait()
+
+    @pl.when(core == 1)
+    def _():
+        pl.semaphore_wait(entered.at[3], 1)
+        start(own_sends(False)[2])
+
+    @pl.when(xpos == 0)
+    def _():
+        pl.semaphore_wait(entered.at[0], 1)
+        start(own_sends(False)[0])
+
+    @pl.when(ypos == 0)
+    def _():
+        pl.semaphore_wait(entered.at[1], 1)
+        start(own_sends(False)[1])
+
+    @pl.when(has_up)
+    def _():
+        pl.semaphore_wait(entered.at[2], 1)
+        start(own_z(ALONG_UP, False))
+
     for copy in scalar_in:
         copy.wait()
     for s in range(sectors):
@@ -328,30 +352,6 @@
             value = jnp.where(lsec[p] == s, p, value)
         inverse[s] = value
         right_of[s] = rsec[value]
-
-    own_r.wait()
-    for copy in own_l:
-        copy.wait()
-
-    @pl.when(core == 1)
-    def _():
-        pl.semaphore_wait(entered.at[3], 1)
-        start(own_sends(False)[2])
-
-    @pl.when(xpos == 0)
-    def _():
-        pl.semaphore_wait(entered.at[0], 1)
-        start(own_sends(False)[0])
-
-    @pl.when(ypos == 0)
-    def _():
-        pl.semaphore_wait(entered.at[1], 1)
-        start(own_sends(False)[1])
-
-    @pl.when(has_up)
-    def _():
-        pl.semaphore_wait(entered.at[2], 1)
-        start(own_z(ALONG_UP, False))
 
     row_at = lax.broadcasted_iota(jnp.int32, (width, width), 0)
     col_at = lax.broadcasted_iota(jnp.int32, (width, width), 1)

time: 25.7 us -> 25.7 us (level)
  no operation moved by 1% of the time
where the time goes in v6:
time: 25.7 us; the launch traced here: 25.6 us
  Pallas kernels  24.6 us (96%)
  local copies, waits for them, and re-layouts  0.97 us (4%)
    pallas_call x1, Pallas kernels, local_shards(): pl.pallas_call(gather_contract, out_shape=pltpu.VMEM(wavefunction.shape,...  24.6 us
    unnamed x1, local copies, waits for them, and re-layouts  0.97 us

profile of v6, /device:TPU:1, one launch (start us, length us, event | category | flops | bytes accessed | tf_op | source)
XLA Modules:
  0.0 25.6 jit_solution(8052409866981675053)
XLA Ops:
  0.0 24.6 %shard_map.73 = f32[16,128,128]{2,1,0:T(8,128)S(1)} custom-call(f32[16,128,128]{2,1,0:T(8,128)} %wf_hbm.1, f32[2,1,128,128]{3,2,1,0:T(8,128)} %lops_hbm.1, f32[2,1,128,128]{3,2,1,0:T(8,128)} %rops_hbm.1, s32[16]{0:T(128)} %lsec_hbm.1, s32[16]{0:T(128)} %rsec_hbm.1, s32[16]{0:T(128)} %lsize_hbm.1, s32[2]{0:T(128)} %rsize_hbm.1), custom_call_target="tpu_custom_call" | custom-call | tf_op jit(solution)/shard_map/pallas_call | solution.py:467
  24.6 1.0 %copy.9 = f32[16,128,128]{2,1,0:T(8,128)} copy(f32[16,128,128]{2,1,0:T(8,128)S(1)} %shard_map.73) | data formatting | bytes 2097152
